TPU v7x, 256 devices: a whole 4x4x8 slice. The times are simulated.
256 devices in a mesh: dp: 32 (over z, y), tensor: 8 (over x, core).
Axes of the slice: x: 4, y: 4, z: 8, core: 2. Of those that a mesh axis runs over, the one named last changes fastest.
Arguments:
- hidden: bfloat16 [4096, 26624], P('dp', 'tensor'), may hold values from -6 to 6
- out_grad: bfloat16 [4096, 8192], P(('dp', 'tensor')), may hold values from -0.375 to 0.375
- master: float32 [8192, 26624], P('dp', 'tensor'), may hold values from -0.3125 to 0.3125
- first_moment: bfloat16 [8192, 26624], P('dp', 'tensor'), may hold values from -4 to 4
- second_moment: bfloat16 [8192, 26624], P('dp', 'tensor'), may hold values from 0.049804688 to 1
- row_counts: int32 [8], replicated, may hold values from 2816 to 3840, as said below
- step_count: int32 [1], replicated, may hold values from 1 to 11
Outputs:
- adam_update: float32 [8192, 26624], P('dp', 'tensor')
- weights_tp: bfloat16 [8192, 30720], P('dp', 'tensor')
Inputs may be any that keep to these rules, and one draw needn't show every extreme that they name: Tensor index j takes row_counts[j] consecutive hidden units in order; they sum to 26624; offsets[j] differs from j * 3328 by at most 256; the largest count equals 3840.
All inputs are finite; a program needn't handle non-finite values.
Results may differ from a plain program's by a relative error of at most 0.0045.
Values may be sent and summed in bfloat16 or wider, within the bound.
No kernel may reach another device: no remote copies, remote signals or barrier semaphores. Data moves between devices by JAX's collectives and lax.ppermute only.
A program may use at most 192 MiB of HBM per device.

v0:
```python
import math
import jax
import jax.numpy as jnp
from jax import lax
from jax.sharding import PartitionSpec as P

DRIFT = 256
CAP = 3840
beta_first = 0.9
beta_second = 0.95
epsilon = 1e-08
decay_rate = 0.1
learn_rate = 0.001


def extended(cells, sides, width):
    for axis, dim in sides:
        count = lax.axis_size(axis)
        ends = count - 1
        head = lax.slice_in_dim(cells, 0, width, axis=dim)
        tail = lax.slice_in_dim(cells, cells.shape[dim] - width, cells.shape[dim], axis=dim)
        cells = jnp.concatenate(
            [
                lax.ppermute(tail, axis, [(i, (i + 1) % count) for i in range(ends)]),
                cells,
                lax.ppermute(head, axis, [((i + 1) % count, i) for i in range(ends)]),
            ],
            axis=dim,
        )
    return cells


def adamw(gradient, master, first_moment, second_moment, steps_done):
    first_new = beta_first * first_moment + (1.0 - beta_first) * gradient
    second_new = beta_second * second_moment + (1.0 - beta_second) * gradient * gradient
    first_fix = 1.0 - jnp.power(beta_first, steps_done)
    second_fix = 1.0 - jnp.power(beta_second, steps_done)
    update = (
        first_new / first_fix / (jnp.sqrt(second_new / second_fix) + epsilon) + decay_rate * master
    )
    master_new = master - learn_rate * update
    return (master_new, update)


def relayout(weights, row_counts):
    shard_rows = weights.shape[0]
    shard_width = weights.shape[1]
    offsets = jnp.cumsum(row_counts) - row_counts
    position = lax.axis_index("tensor")
    first_slot = lax.dynamic_index_in_dim(offsets, position, keepdims=False)
    length = lax.dynamic_index_in_dim(row_counts, position, keepdims=False)
    padded = extended(weights, (("tensor", 1),), DRIFT)
    widened = jnp.concatenate([padded, jnp.zeros((shard_rows, 2 * DRIFT), jnp.bfloat16)], axis=1)
    start = first_slot - position * shard_width + DRIFT
    window = lax.dynamic_slice_in_dim(widened, start, CAP, 1)
    slot_index = jnp.arange(CAP, dtype=jnp.int32)
    return jnp.where((slot_index < length)[None, :], window, jnp.zeros((), jnp.bfloat16))


def per_device(hidden, out_grad, master, first_moment, second_moment, row_counts, step_count):
    shard_rows = master.shape[0]
    hidden_units = hidden.shape[1]
    regrouped = lax.all_to_all(out_grad, "dp", split_axis=1, concat_axis=0, tiled=True)
    spread = lax.all_gather(regrouped, "tensor", axis=0, tiled=True)
    tensor_count = lax.axis_size("tensor")
    data_count = lax.axis_size("dp")
    local_tokens = out_grad.shape[0]
    group_tokens = hidden.shape[0]
    owned_cols = spread.reshape(tensor_count, data_count, local_tokens, shard_rows)
    shard_piece = lax.all_gather(hidden, "dp", axis=0, tiled=True)
    groups = shard_piece.shape[0] // group_tokens
    per_turn = math.gcd(groups, 4)
    turns = groups // per_turn
    activations = shard_piece.reshape(groups, tensor_count, local_tokens, hidden_units)

    def one_turn(turn_index, running):
        grad_block = lax.dynamic_slice_in_dim(owned_cols, turn_index * per_turn, per_turn, 1)
        act_block = lax.dynamic_slice_in_dim(activations, turn_index * per_turn, per_turn, 0)
        partial_value = jnp.einsum(
            "tgrd,gtrf->gdf", grad_block, act_block, preferred_element_type=jnp.float32
        )
        rounded = lax.optimization_barrier(partial_value.astype(jnp.bfloat16)).astype(jnp.float32)
        return running + jnp.sum(rounded, axis=0)

    gradient = lax.fori_loop(0, turns, one_turn, jnp.zeros((shard_rows, hidden_units), jnp.float32))
    steps_done = step_count[0].astype(jnp.float32)
    master_new, update = adamw(
        gradient,
        master,
        first_moment.astype(jnp.float32),
        second_moment.astype(jnp.float32),
        steps_done,
    )
    laid = relayout(master_new.astype(jnp.bfloat16), row_counts)
    outputs = [(update, laid)]
    joined = [jnp.concatenate([entry[slot] for entry in outputs], axis=0) for slot in range(2)]
    return (joined[0], joined[1])


def solution(mesh):
    return jax.shard_map(
        per_device,
        mesh=mesh,
        in_specs=(
            P("dp", "tensor"),
            P(("dp", "tensor"), None),
            P("dp", "tensor"),
            P("dp", "tensor"),
            P("dp", "tensor"),
            P(),
            P(),
        ),
        out_specs=(P("dp", "tensor"), P("dp", "tensor")),
        check_vma=False,
    )
```

profile of v0, /device:TPU:1, one launch (start us, length us, event | category | flops | bytes accessed | tf_op | source)
XLA Modules:
  0.0 353.1 jit_solution(3971043392902554566)
XLA Ops:
  7.2 0.0 all-gather.3.cloned.1.call-start
  7.2 1.0 copy.20
  8.2 23.1 %all_to_all.19 = bf16[16,32,256]{2,0,1:T(8,128)(2,1)} all-to-all(bf16[16,32,256]{2,0,1:T(8,128)(2,1)S(1)} %bitcast.22), channel_id=1, replica_groups=mesh['dp'=32,'tensor'=8] {'dp'}, dimensions={1} | all-to-all | bytes 524288 | tf_op jit(solution)/shard_map/all_to_all | solution.py:63
  31.3 0.0 all-gather.3.cloned.1.call-update
  31.3 0.0 all-gather.5.cloned.1.call-start
  31.4 0.7 all-gather.5.cloned.1.call-update
  32.8 0.8 reduce-window.9
  33.7 1.2 dynamic_slice.24
  34.9 0.7 bitcast_subtract_fusion
  35.6 21.4 %all-gather.3.cloned.1.call-done = bf16[4096,256]{1,0:T(8,128)(2,1)} async-done(((bf16[512,256]{1,0:T(8,128)(2,1)}), bf16[4096,256]{1,0:T(8,128)(2,1)}) %all-gather.3.cloned.1.call-update) | async-done | bytes 2097168 | tf_op jit(solution)/shard_map/all_gather | solution.py:64
  56.9 198.3 %all-gather.5.cloned.1.call-done = bf16[4096,3328]{1,0:T(8,128)(2,1)} async-done(((bf16[128,3328]{1,0:T(8,128)(2,1)}), bf16[4096,3328]{1,0:T(8,128)(2,1)}) %all-gather.5.cloned.1.call-update) | async-done | bytes 27262992 | tf_op jit(solution)/shard_map/all_gather | solution.py:70
  255.3 71.0 %while.14 = (s32[]{:T(128)}, f32[256,3328]{1,0:T(8,128)}, bf16[8,32,16,256]{3,2,1,0:T(8,128)(2,1)}, bf16[32,8,16,3328]{3,2,1,0:T(8,128)(2,1)}, s32[]{:T(128)}, /*index=5*/s32[]{:T(128)}, s32[]{:T(128)}, s32[]{:T(128)}) while((s32[]{:T(128)}, f32[256,3328]{1,0:T(8,128)}, bf16[8,32,16,256]{3,2,1,0:T(8,128)(2,1)}, ...), condition=%wide.region_2.0_spmd.clone, body=%wide.region_0.0_spmd.clone.sunk | while | flops 883490816 | bytes 30934164 | solution.py:85
  255.3 4.0 %bitcast_convert_fusion.2 = bf16[4,256,3328]{2,1,0:T(8,128)(2,1)S(1)} fusion(bf16[32,8,16,3328]{3,2,1,0:T(8,128)(2,1)} %get-tuple-element.165, s32[]{:T(128)S(6)} %select_n.26, bf16[8,32,16,256]{3,2,1,0:T(8,128)(2,1)} %get-tuple-element.164), kind=kOutput, calls=%fused_computation.clone.1 | convolution fusion | flops 875823104 | bytes 10486784 | tf_op jit(solution)/shard_map/while/body/eval_jaxpr/tgrd,gtrf->gdf/dot_general | solution.py:79
  259.3 1.0 convert_reduce_fusion.2
  260.3 2.1 select_add_fusion.2
  262.4 4.0 %bitcast_convert_fusion.2 = bf16[4,256,3328]{2,1,0:T(8,128)(2,1)S(1)} fusion(bf16[32,8,16,3328]{3,2,1,0:T(8,128)(2,1)} %get-tuple-element.165, s32[]{:T(128)S(6)} %select_n.26, bf16[8,32,16,256]{3,2,1,0:T(8,128)(2,1)} %get-tuple-element.164), kind=kOutput, calls=%fused_computation.clone.1 | convolution fusion | flops 875823104 | bytes 10486784 | tf_op jit(solution)/shard_map/while/body/eval_jaxpr/tgrd,gtrf->gdf/dot_general | solution.py:79
  266.4 1.0 convert_reduce_fusion.2
  267.4 4.1 %select_add_fusion.2 = f32[256,3328]{1,0:T(8,128)} fusion(f32[256,3328]{1,0:T(8,128)S(1)} %convert_reduce_fusion.2, f32[256,3328]{1,0:T(8,128)} %get-tuple-element.155, pred[]{:T(512)S(6)} %compare.3), kind=kLoop, calls=%fused_computation.2.clone.1 | loop fusion | flops 1703936 | bytes 10223617 | tf_op jit(solution)/shard_map/while/body/eval_jaxpr/add | solution.py:83
  271.5 4.0 %bitcast_convert_fusion.2 = bf16[4,256,3328]{2,1,0:T(8,128)(2,1)S(1)} fusion(bf16[32,8,16,3328]{3,2,1,0:T(8,128)(2,1)} %get-tuple-element.165, s32[]{:T(128)S(6)} %select_n.26, bf16[8,32,16,256]{3,2,1,0:T(8,128)(2,1)} %get-tuple-element.164), kind=kOutput, calls=%fused_computation.clone.1 | convolution fusion | flops 875823104 | bytes 10486784 | tf_op jit(solution)/shard_map/while/body/eval_jaxpr/tgrd,gtrf->gdf/dot_general | solution.py:79
  275.6 1.0 convert_reduce_fusion.2
  276.6 4.1 %select_add_fusion.2 = f32[256,3328]{1,0:T(8,128)} fusion(f32[256,3328]{1,0:T(8,128)S(1)} %convert_reduce_fusion.2, f32[256,3328]{1,0:T(8,128)} %get-tuple-element.155, pred[]{:T(512)S(6)} %compare.3), kind=kLoop, calls=%fused_computation.2.clone.1 | loop fusion | flops 1703936 | bytes 10223617 | tf_op jit(solution)/shard_map/while/body/eval_jaxpr/add | solution.py:83
  280.7 4.0 %bitcast_convert_fusion.2 = bf16[4,256,3328]{2,1,0:T(8,128)(2,1)S(1)} fusion(bf16[32,8,16,3328]{3,2,1,0:T(8,128)(2,1)} %get-tuple-element.165, s32[]{:T(128)S(6)} %select_n.26, bf16[8,32,16,256]{3,2,1,0:T(8,128)(2,1)} %get-tuple-element.164), kind=kOutput, calls=%fused_computation.clone.1 | convolution fusion | flops 875823104 | bytes 10486784 | tf_op jit(solution)/shard_map/while/body/eval_jaxpr/tgrd,gtrf->gdf/dot_general | solution.py:79
  284.7 1.0 convert_reduce_fusion.2
  285.7 4.1 %select_add_fusion.2 = f32[256,3328]{1,0:T(8,128)} fusion(f32[256,3328]{1,0:T(8,128)S(1)} %convert_reduce_fusion.2, f32[256,3328]{1,0:T(8,128)} %get-tuple-element.155, pred[]{:T(512)S(6)} %compare.3), kind=kLoop, calls=%fused_computation.2.clone.1 | loop fusion | flops 1703936 | bytes 10223617 | tf_op jit(solution)/shard_map/while/body/eval_jaxpr/add | solution.py:83
  289.8 4.0 %bitcast_convert_fusion.2 = bf16[4,256,3328]{2,1,0:T(8,128)(2,1)S(1)} fusion(bf16[32,8,16,3328]{3,2,1,0:T(8,128)(2,1)} %get-tuple-element.165, s32[]{:T(128)S(6)} %select_n.26, bf16[8,32,16,256]{3,2,1,0:T(8,128)(2,1)} %get-tuple-element.164), kind=kOutput, calls=%fused_computation.clone.1 | convolution fusion | flops 875823104 | bytes 10486784 | tf_op jit(solution)/shard_map/while/body/eval_jaxpr/tgrd,gtrf->gdf/dot_general | solution.py:79
  293.8 1.0 convert_reduce_fusion.2
  294.8 4.1 %select_add_fusion.2 = f32[256,3328]{1,0:T(8,128)} fusion(f32[256,3328]{1,0:T(8,128)S(1)} %convert_reduce_fusion.2, f32[256,3328]{1,0:T(8,128)} %get-tuple-element.155, pred[]{:T(512)S(6)} %compare.3), kind=kLoop, calls=%fused_computation.2.clone.1 | loop fusion | flops 1703936 | bytes 10223617 | tf_op jit(solution)/shard_map/while/body/eval_jaxpr/add | solution.py:83
  298.9 4.0 %bitcast_convert_fusion.2 = bf16[4,256,3328]{2,1,0:T(8,128)(2,1)S(1)} fusion(bf16[32,8,16,3328]{3,2,1,0:T(8,128)(2,1)} %get-tuple-element.165, s32[]{:T(128)S(6)} %select_n.26, bf16[8,32,16,256]{3,2,1,0:T(8,128)(2,1)} %get-tuple-element.164), kind=kOutput, calls=%fused_computation.clone.1 | convolution fusion | flops 875823104 | bytes 10486784 | tf_op jit(solution)/shard_map/while/body/eval_jaxpr/tgrd,gtrf->gdf/dot_general | solution.py:79
  302.9 1.0 convert_reduce_fusion.2
  303.9 4.1 %select_add_fusion.2 = f32[256,3328]{1,0:T(8,128)} fusion(f32[256,3328]{1,0:T(8,128)S(1)} %convert_reduce_fusion.2, f32[256,3328]{1,0:T(8,128)} %get-tuple-element.155, pred[]{:T(512)S(6)} %compare.3), kind=kLoop, calls=%fused_computation.2.clone.1 | loop fusion | flops 1703936 | bytes 10223617 | tf_op jit(solution)/shard_map/while/body/eval_jaxpr/add | solution.py:83
  308.0 4.0 %bitcast_convert_fusion.2 = bf16[4,256,3328]{2,1,0:T(8,128)(2,1)S(1)} fusion(bf16[32,8,16,3328]{3,2,1,0:T(8,128)(2,1)} %get-tuple-element.165, s32[]{:T(128)S(6)} %select_n.26, bf16[8,32,16,256]{3,2,1,0:T(8,128)(2,1)} %get-tuple-element.164), kind=kOutput, calls=%fused_computation.clone.1 | convolution fusion | flops 875823104 | bytes 10486784 | tf_op jit(solution)/shard_map/while/body/eval_jaxpr/tgrd,gtrf->gdf/dot_general | solution.py:79
  312.0 1.0 convert_reduce_fusion.2
  313.1 4.1 %select_add_fusion.2 = f32[256,3328]{1,0:T(8,128)} fusion(f32[256,3328]{1,0:T(8,128)S(1)} %convert_reduce_fusion.2, f32[256,3328]{1,0:T(8,128)} %get-tuple-element.155, pred[]{:T(512)S(6)} %compare.3), kind=kLoop, calls=%fused_computation.2.clone.1 | loop fusion | flops 1703936 | bytes 10223617 | tf_op jit(solution)/shard_map/while/body/eval_jaxpr/add | solution.py:83
  317.1 4.0 %bitcast_convert_fusion.2 = bf16[4,256,3328]{2,1,0:T(8,128)(2,1)S(1)} fusion(bf16[32,8,16,3328]{3,2,1,0:T(8,128)(2,1)} %get-tuple-element.165, s32[]{:T(128)S(6)} %select_n.26, bf16[8,32,16,256]{3,2,1,0:T(8,128)(2,1)} %get-tuple-element.164), kind=kOutput, calls=%fused_computation.clone.1 | convolution fusion | flops 875823104 | bytes 10486784 | tf_op jit(solution)/shard_map/while/body/eval_jaxpr/tgrd,gtrf->gdf/dot_general | solution.py:79
  321.2 1.0 convert_reduce_fusion.2
  322.2 4.1 %select_add_fusion.2 = f32[256,3328]{1,0:T(8,128)} fusion(f32[256,3328]{1,0:T(8,128)S(1)} %convert_reduce_fusion.2, f32[256,3328]{1,0:T(8,128)} %get-tuple-element.155, pred[]{:T(512)S(6)} %compare.3), kind=kLoop, calls=%fused_computation.2.clone.1 | loop fusion | flops 1703936 | bytes 10223617 | tf_op jit(solution)/shard_map/while/body/eval_jaxpr/add | solution.py:83
  326.3 6.5 %subtract_convert_fusion = (bf16[256,3328]{1,0:T(8,128)(2,1)S(1)}, f32[256,3328]{1,0:T(8,128)}) fusion(f32[256,3328]{1,0:T(8,128)} %param.11, f32[]{:T(128)} %bitcast.5, f32[256,3328]{1,0:T(8,128)} %get-tuple-element.81, bf16[256,3328]{1,0:T(8,128)(2,1)} %param.13, f32[]{:T(128)} %bitcast.4, bf16[256,3328]{1,0:T(8,128)(2,1)} %param.12), kind=kLoop, calls=%fused_computation.14 | loop fusion | flops 15335424 | bytes 15335432 | tf_op jit(solution)/shard_map/convert_element_type | solution.py:94
  332.8 4.0 %collective-permute-start = (bf16[256,256]{1,0:T(8,128)(2,1)S(1)}, bf16[256,256]{1,0:T(8,128)(2,1)S(1)}, u32[]{:S(2)}, u32[]{:S(2)}) collective-permute-start(bf16[256,256]{1,0:T(8,128)(2,1)S(1)} %get-tuple-element.120), channel_id=1, source_target_pairs={{0,1},{1,2},{2,3},{3,4},{4,5},{5,6},{6,7},{8,9},{9,10},{10,11},{11... | collective-permute-start | bytes 393224 | tf_op jit(solution)/shard_map/ppermute | solution.py:24
  336.8 1.9 collective-permute-start.1
  338.7 0.6 iota_compare_fusion
  339.4 0.6 dynamic_slice.25
  340.6 0.1 pad_dynamic-slice_fusion.3
  340.7 0.0 collective-permute-done
  340.7 2.4 collective-permute-done.1
  343.1 3.1 fusion.12
  (3 shorter events, 0.0 us)
Async XLA Ops:
  7.2 49.8 %all-gather.3.cloned.1.call-start = ((), (), s32[]{:S(2)}) async-start(), calls=%async_computation.1 | async-start | bytes 2359296 | tf_op jit(solution)/shard_map/all_gather | solution.py:64
  31.3 223.9 %all-gather.5.cloned.1.call-start = ((), (), s32[]{:S(2)}) async-start(), calls=%async_computation.2 | async-start | bytes 28114944 | tf_op jit(solution)/shard_map/all_gather | solution.py:70
  332.8 7.9 %collective-permute-start = (bf16[256,256]{1,0:T(8,128)(2,1)S(1)}, bf16[256,256]{1,0:T(8,128)(2,1)S(1)}, u32[]{:S(2)}, u32[]{:S(2)}) collective-permute-start(bf16[256,256]{1,0:T(8,128)(2,1)S(1)} %get-tuple-element.120), channel_id=1, source_target_pairs={{0,1},{1,2},{2,3},{3,4},{4,5},{5,6},{6,7},{8,9},{9,10},{10,11},{11... | collective-permute-start | bytes 393224 | tf_op jit(solution)/shard_map/ppermute | solution.py:24
  336.8 6.3 %collective-permute-start.1 = (bf16[256,256]{1,0:T(8,128)(2,1)S(1)}, bf16[256,256]{1,0:T(8,128)(2,1)S(1)}, u32[]{:S(2)}, u32[]{:S(2)}) collective-permute-start(bf16[256,256]{1,0:T(8,128)(2,1)S(1)} %get-tuple-element.119), channel_id=1, source_target_pairs={{1,0},{2,1},{3,2},{4,3},{5,4},{6,5},{7,6},{9,8},{10,9},{11,10},{12... | collective-permute-start | bytes 393224 | tf_op jit(solution)/shard_map/ppermute | solution.py:26
Sparse Core Ops, SparseCore 0:
  31.5 25.4 all-gather.2
  59.5 195.6 all-gather.4
where the time goes:
time: 354 us; the launch traced here: 353 us
  waiting for transfers between devices  223 us (63%)
  other arithmetic  50.5 us (14%)
  matrix products  32.1 us (9%)
  blocking collectives  23.1 us (7%)
  between operations  15.5 us (4%)
  starting transfers between devices  6.03 us (2%)
    all_gather x1, waiting for transfers between devices, per_device(): shard_piece = lax.all_gather(hidden, 'dp', axis=0, tiled=True)  198 us
    dot_general x8, matrix products, one_turn(): jnp.einsum('tgrd,gtrf->gdf', grad_block, act_block, preferred_element_typ...  32.1 us
    add x8, other arithmetic, one_turn(): return running + jnp.sum(rounded, axis=0)  30.8 us
    all_to_all x1, blocking collectives, per_device(): lax.all_to_all(out_grad, 'dp', split_axis=1, concat_axis=0, tiled=True)  23.1 us
    all_gather x1, waiting for transfers between devices, per_device(): spread = lax.all_gather(regrouped, 'tensor', axis=0, tiled=True)  21.4 us
    reduce_sum x8, other arithmetic, one_turn(): return running + jnp.sum(rounded, axis=0)  7.96 us
  transfers between devices with their start and end apart: 4, of which 3 were waited for; matrix products, arithmetic and copies ran while one was open for 1% of the time, Pallas kernels for 0%

commit v1 on v0

--- a/solution.py
+++ b/solution.py
@@ -11,6 +11,28 @@
 epsilon = 1e-08
 decay_rate = 0.1
 learn_rate = 0.001
+
+
+def in_order(blocks, dim):
+    blocks = jnp.moveaxis(blocks, 0, dim)
+    dims = blocks.shape
+    return blocks.reshape(*dims[:dim], dims[dim] * dims[dim + 1], *dims[dim + 2 :])
+
+
+def ring_gather(shard, axis, dim):
+    length = lax.axis_size(axis)
+    pairs = [(i, (i + 1) % length) for i in range(length)]
+    back = [(b, a) for a, b in pairs]
+    lower, upper = ([], [])
+    for turn in range(length - 1):
+        if turn % 2 == 0:
+            lower.append(lax.ppermute(lower[-1] if lower else shard, axis, pairs))
+        else:
+            upper.append(lax.ppermute(upper[-1] if upper else shard, axis, back))
+    pieces = jnp.stack([*lower[::-1], shard, *upper])
+    shift = lax.axis_index(axis) - len(lower)
+    pieces = pieces[(jnp.arange(length) - shift) % length]
+    return in_order(pieces, dim)
 
 
 def extended(cells, sides, width):
@@ -61,7 +83,7 @@
     shard_rows = master.shape[0]
     hidden_units = hidden.shape[1]
     regrouped = lax.all_to_all(out_grad, "dp", split_axis=1, concat_axis=0, tiled=True)
-    spread = lax.all_gather(regrouped, "tensor", axis=0, tiled=True)
+    spread = ring_gather(regrouped, "tensor", 0)
     tensor_count = lax.axis_size("tensor")
     data_count = lax.axis_size("dp")
     local_tokens = out_grad.shape[0]

time: 354 us -> 309 us (0.87)
  waiting for transfers between devices: 223 us -> 159 us
  starting transfers between devices: 6.03 us -> 20.7 us
  local copies, waits for them, and re-layouts: 2.92 us -> 7.01 us
    all_gather x1, waiting for transfers between devices: 198 us -> 145 us  [per_device(): shard_piece = lax.all_gather(hidden, 'dp', axis=0, tiled=True)]
    all_gather x1 -> x0, waiting for transfers between devices: 21.4 us -> none  [per_device(): spread = lax.all_gather(regrouped, 'tensor', axis=0, tiled=True)]
    ppermute x0 -> x7, starting transfers between devices: none -> 14.7 us  [the longest x4 11.1 us: ring_gather(): lower.append(lax.ppermute(lower[-1] if lower else shard, axis, pairs))]
    ppermute x0 -> x7, waiting for transfers between devices: none -> 10.6 us  [the longest x4 8.47 us: ring_gather(): lower.append(lax.ppermute(lower[-1] if lower else shard, axis, pairs))]
  transfers between devices with their start and end apart: 4 -> 10, of which waited for: 3 -> 7; matrix products, arithmetic and copies ran while one was open for 1% -> 3% of each run, Pallas kernels for 0% -> 0%
where the time goes in v1:
time: 309 us; the launch traced here: 308 us
  waiting for transfers between devices  159 us (51%)
  other arithmetic  50.5 us (16%)
  matrix products  32.1 us (10%)
  blocking collectives  23 us (7%)
  starting transfers between devices  20.7 us (7%)
  between operations  15.5 us (5%)
  local copies, waits for them, and re-layouts  7.01 us (2%)
    all_gather x1, waiting for transfers between devices, per_device(): shard_piece = lax.all_gather(hidden, 'dp', axis=0, tiled=True)  145 us
    dot_general x8, matrix products, one_turn(): jnp.einsum('tgrd,gtrf->gdf', grad_block, act_block, preferred_element_typ...  32.1 us
    add x8, other arithmetic, one_turn(): return running + jnp.sum(rounded, axis=0)  30.8 us
    all_to_all x1, blocking collectives, per_device(): lax.all_to_all(out_grad, 'dp', split_axis=1, concat_axis=0, tiled=True)  23 us
    ppermute x4, starting transfers between devices, ring_gather(): lower.append(lax.ppermute(lower[-1] if lower else shard, axis, pairs))  11.1 us
    ppermute x4, waiting for transfers between devices, ring_gather(): lower.append(lax.ppermute(lower[-1] if lower else shard, axis, pairs))  8.47 us
    reduce_sum x8, other arithmetic, one_turn(): return running + jnp.sum(rounded, axis=0)  7.96 us
    convert_element_type x1, other arithmetic, per_device(): laid = relayout(master_new.astype(jnp.bfloat16), row_counts)  6.5 us
  transfers between devices with their start and end apart: 10, of which 7 were waited for; matrix products, arithmetic and copies ran while one was open for 3% of the time, Pallas kernels for 0%

profile of v1, /device:TPU:1, one launch (start us, length us, event | category | flops | bytes accessed | tf_op | source)
XLA Modules:
  0.0 308.0 jit_solution(16727883591767059211)
XLA Ops:
  7.9 1.0 copy.21
  8.9 23.0 %all_to_all.19 = bf16[16,32,256]{2,0,1:T(8,128)(2,1)S(1)} all-to-all(bf16[16,32,256]{2,0,1:T(8,128)(2,1)S(1)} %bitcast.43), channel_id=1, replica_groups=mesh['dp'=32,'tensor'=8] {'dp'}, dimensions={1} | all-to-all | bytes 524288 | tf_op jit(solution)/shard_map/all_to_all | solution.py:85
  31.9 3.7 %collective-permute-start = (bf16[512,256]{1,0:T(8,128)(2,1)S(1)}, bf16[512,256]{1,0:T(8,128)(2,1)S(1)}, u32[]{:S(2)}, u32[]{:S(2)}) collective-permute-start(bf16[512,256]{1,0:T(8,128)(2,1)S(1)} %bitcast.40), channel_id=1, source_target_pairs={{0,1},{1,2},{2,3},{3,4},{4,5},{5,6},{6,7},{7,0},{8,9},{9,10},{10,1... | collective-permute-start | bytes 786440 | tf_op jit(solution)/shard_map/ppermute | solution.py:29
  35.5 3.3 %collective-permute-done = bf16[512,256]{1,0:T(8,128)(2,1)S(1)} collective-permute-done((bf16[512,256]{1,0:T(8,128)(2,1)S(1)}, bf16[512,256]{1,0:T(8,128)(2,1)S(1)}, u32[]{:S(2)}, u32[]{:S(2)}) %collective-permute-start) | collective-permute-done | bytes 262176 | tf_op jit(solution)/shard_map/ppermute | solution.py:29
  38.9 2.5 collective-permute-start.1
  41.5 3.2 %collective-permute-done.1 = bf16[512,256]{1,0:T(8,128)(2,1)S(1)} collective-permute-done((bf16[512,256]{1,0:T(8,128)(2,1)S(1)}, bf16[512,256]{1,0:T(8,128)(2,1)S(1)}, u32[]{:S(2)}, u32[]{:S(2)}) %collective-permute-start.1) | collective-permute-done | bytes 262176 | tf_op jit(solution)/shard_map/ppermute | solution.py:29
  44.7 2.5 collective-permute-start.2
  47.5 1.0 collective-permute-start.5
  48.5 2.0 collective-permute-done.2
  50.5 2.5 collective-permute-start.3
  53.7 0.8 reduce-window.9
  54.5 1.3 dynamic_slice.24
  56.4 2.5 collective-permute-start.6
  59.0 1.0 bitcast_dynamic-update-slice_fusion.6
  60.1 1.0 bitcast_dynamic-update-slice_fusion.1
  61.1 1.8 collective-permute-done.6
  62.9 2.0 gather_fusion
  64.9 145.3 %all-gather.2.cloned.1.call-done = bf16[4096,3328]{1,0:T(8,128)(2,1)} async-done(((bf16[128,3328]{1,0:T(8,128)(2,1)}), bf16[4096,3328]{1,0:T(8,128)(2,1)}) %all-gather.2.cloned.1.call-update) | async-done | bytes 27262992 | tf_op jit(solution)/shard_map/all_gather | solution.py:92
  210.2 71.0 %while.14 = (s32[]{:T(128)}, f32[256,3328]{1,0:T(8,128)}, bf16[8,32,16,256]{3,2,1,0:T(8,128)(2,1)}, bf16[32,8,16,3328]{3,2,1,0:T(8,128)(2,1)}, s32[]{:T(128)}, /*index=5*/s32[]{:T(128)}, s32[]{:T(128)}, s32[]{:T(128)}) while((s32[]{:T(128)}, f32[256,3328]{1,0:T(8,128)}, bf16[8,32,16,256]{3,2,1,0:T(8,128)(2,1)}, ...), condition=%wide.region_2.3_spmd.clone, body=%wide.region_0.2_spmd.clone.sunk | while | flops 883490816 | bytes 30934164 | solution.py:107
  210.2 4.0 %bitcast_convert_fusion.2 = bf16[4,256,3328]{2,1,0:T(8,128)(2,1)S(1)} fusion(bf16[32,8,16,3328]{3,2,1,0:T(8,128)(2,1)} %get-tuple-element.165, s32[]{:T(128)S(6)} %select_n.60, bf16[8,32,16,256]{3,2,1,0:T(8,128)(2,1)} %get-tuple-element.164), kind=kOutput, calls=%fused_computation.1.clone.1 | convolution fusion | flops 875823104 | bytes 10486784 | tf_op jit(solution)/shard_map/while/body/eval_jaxpr/tgrd,gtrf->gdf/dot_general | solution.py:101
  214.2 1.0 convert_reduce_fusion.2
  215.2 2.1 select_add_fusion.2
  217.3 4.0 %bitcast_convert_fusion.2 = bf16[4,256,3328]{2,1,0:T(8,128)(2,1)S(1)} fusion(bf16[32,8,16,3328]{3,2,1,0:T(8,128)(2,1)} %get-tuple-element.165, s32[]{:T(128)S(6)} %select_n.60, bf16[8,32,16,256]{3,2,1,0:T(8,128)(2,1)} %get-tuple-element.164), kind=kOutput, calls=%fused_computation.1.clone.1 | convolution fusion | flops 875823104 | bytes 10486784 | tf_op jit(solution)/shard_map/while/body/eval_jaxpr/tgrd,gtrf->gdf/dot_general | solution.py:101
  221.4 1.0 convert_reduce_fusion.2
  222.4 4.1 %select_add_fusion.2 = f32[256,3328]{1,0:T(8,128)} fusion(f32[256,3328]{1,0:T(8,128)S(1)} %convert_reduce_fusion.2, f32[256,3328]{1,0:T(8,128)} %get-tuple-element.155, pred[]{:T(512)S(6)} %compare.10), kind=kLoop, calls=%fused_computation.3.clone.1 | loop fusion | flops 1703936 | bytes 10223617 | tf_op jit(solution)/shard_map/while/body/eval_jaxpr/add | solution.py:105
  226.5 4.0 %bitcast_convert_fusion.2 = bf16[4,256,3328]{2,1,0:T(8,128)(2,1)S(1)} fusion(bf16[32,8,16,3328]{3,2,1,0:T(8,128)(2,1)} %get-tuple-element.165, s32[]{:T(128)S(6)} %select_n.60, bf16[8,32,16,256]{3,2,1,0:T(8,128)(2,1)} %get-tuple-element.164), kind=kOutput, calls=%fused_computation.1.clone.1 | convolution fusion | flops 875823104 | bytes 10486784 | tf_op jit(solution)/shard_map/while/body/eval_jaxpr/tgrd,gtrf->gdf/dot_general | solution.py:101
  230.5 1.0 convert_reduce_fusion.2
  231.5 4.1 %select_add_fusion.2 = f32[256,3328]{1,0:T(8,128)} fusion(f32[256,3328]{1,0:T(8,128)S(1)} %convert_reduce_fusion.2, f32[256,3328]{1,0:T(8,128)} %get-tuple-element.155, pred[]{:T(512)S(6)} %compare.10), kind=kLoop, calls=%fused_computation.3.clone.1 | loop fusion | flops 1703936 | bytes 10223617 | tf_op jit(solution)/shard_map/while/body/eval_jaxpr/add | solution.py:105
  235.6 4.0 %bitcast_convert_fusion.2 = bf16[4,256,3328]{2,1,0:T(8,128)(2,1)S(1)} fusion(bf16[32,8,16,3328]{3,2,1,0:T(8,128)(2,1)} %get-tuple-element.165, s32[]{:T(128)S(6)} %select_n.60, bf16[8,32,16,256]{3,2,1,0:T(8,128)(2,1)} %get-tuple-element.164), kind=kOutput, calls=%fused_computation.1.clone.1 | convolution fusion | flops 875823104 | bytes 10486784 | tf_op jit(solution)/shard_map/while/body/eval_jaxpr/tgrd,gtrf->gdf/dot_general | solution.py:101
  239.6 1.0 convert_reduce_fusion.2
  240.6 4.1 %select_add_fusion.2 = f32[256,3328]{1,0:T(8,128)} fusion(f32[256,3328]{1,0:T(8,128)S(1)} %convert_reduce_fusion.2, f32[256,3328]{1,0:T(8,128)} %get-tuple-element.155, pred[]{:T(512)S(6)} %compare.10), kind=kLoop, calls=%fused_computation.3.clone.1 | loop fusion | flops 1703936 | bytes 10223617 | tf_op jit(solution)/shard_map/while/body/eval_jaxpr/add | solution.py:105
  244.7 4.0 %bitcast_convert_fusion.2 = bf16[4,256,3328]{2,1,0:T(8,128)(2,1)S(1)} fusion(bf16[32,8,16,3328]{3,2,1,0:T(8,128)(2,1)} %get-tuple-element.165, s32[]{:T(128)S(6)} %select_n.60, bf16[8,32,16,256]{3,2,1,0:T(8,128)(2,1)} %get-tuple-element.164), kind=kOutput, calls=%fused_computation.1.clone.1 | convolution fusion | flops 875823104 | bytes 10486784 | tf_op jit(solution)/shard_map/while/body/eval_jaxpr/tgrd,gtrf->gdf/dot_general | solution.py:101
  248.7 1.0 convert_reduce_fusion.2
  249.7 4.1 %select_add_fusion.2 = f32[256,3328]{1,0:T(8,128)} fusion(f32[256,3328]{1,0:T(8,128)S(1)} %convert_reduce_fusion.2, f32[256,3328]{1,0:T(8,128)} %get-tuple-element.155, pred[]{:T(512)S(6)} %compare.10), kind=kLoop, calls=%fused_computation.3.clone.1 | loop fusion | flops 1703936 | bytes 10223617 | tf_op jit(solution)/shard_map/while/body/eval_jaxpr/add | solution.py:105
  253.8 4.0 %bitcast_convert_fusion.2 = bf16[4,256,3328]{2,1,0:T(8,128)(2,1)S(1)} fusion(bf16[32,8,16,3328]{3,2,1,0:T(8,128)(2,1)} %get-tuple-element.165, s32[]{:T(128)S(6)} %select_n.60, bf16[8,32,16,256]{3,2,1,0:T(8,128)(2,1)} %get-tuple-element.164), kind=kOutput, calls=%fused_computation.1.clone.1 | convolution fusion | flops 875823104 | bytes 10486784 | tf_op jit(solution)/shard_map/while/body/eval_jaxpr/tgrd,gtrf->gdf/dot_general | solution.py:101
  257.9 1.0 convert_reduce_fusion.2
  258.9 4.1 %select_add_fusion.2 = f32[256,3328]{1,0:T(8,128)} fusion(f32[256,3328]{1,0:T(8,128)S(1)} %convert_reduce_fusion.2, f32[256,3328]{1,0:T(8,128)} %get-tuple-element.155, pred[]{:T(512)S(6)} %compare.10), kind=kLoop, calls=%fused_computation.3.clone.1 | loop fusion | flops 1703936 | bytes 10223617 | tf_op jit(solution)/shard_map/while/body/eval_jaxpr/add | solution.py:105
  263.0 4.0 %bitcast_convert_fusion.2 = bf16[4,256,3328]{2,1,0:T(8,128)(2,1)S(1)} fusion(bf16[32,8,16,3328]{3,2,1,0:T(8,128)(2,1)} %get-tuple-element.165, s32[]{:T(128)S(6)} %select_n.60, bf16[8,32,16,256]{3,2,1,0:T(8,128)(2,1)} %get-tuple-element.164), kind=kOutput, calls=%fused_computation.1.clone.1 | convolution fusion | flops 875823104 | bytes 10486784 | tf_op jit(solution)/shard_map/while/body/eval_jaxpr/tgrd,gtrf->gdf/dot_general | solution.py:101
  267.0 1.0 convert_reduce_fusion.2
  268.0 4.1 %select_add_fusion.2 = f32[256,3328]{1,0:T(8,128)} fusion(f32[256,3328]{1,0:T(8,128)S(1)} %convert_reduce_fusion.2, f32[256,3328]{1,0:T(8,128)} %get-tuple-element.155, pred[]{:T(512)S(6)} %compare.10), kind=kLoop, calls=%fused_computation.3.clone.1 | loop fusion | flops 1703936 | bytes 10223617 | tf_op jit(solution)/shard_map/while/body/eval_jaxpr/add | solution.py:105
  272.1 4.0 %bitcast_convert_fusion.2 = bf16[4,256,3328]{2,1,0:T(8,128)(2,1)S(1)} fusion(bf16[32,8,16,3328]{3,2,1,0:T(8,128)(2,1)} %get-tuple-element.165, s32[]{:T(128)S(6)} %select_n.60, bf16[8,32,16,256]{3,2,1,0:T(8,128)(2,1)} %get-tuple-element.164), kind=kOutput, calls=%fused_computation.1.clone.1 | convolution fusion | flops 875823104 | bytes 10486784 | tf_op jit(solution)/shard_map/while/body/eval_jaxpr/tgrd,gtrf->gdf/dot_general | solution.py:101
  276.1 1.0 convert_reduce_fusion.2
  277.1 4.1 %select_add_fusion.2 = f32[256,3328]{1,0:T(8,128)} fusion(f32[256,3328]{1,0:T(8,128)S(1)} %convert_reduce_fusion.2, f32[256,3328]{1,0:T(8,128)} %get-tuple-element.155, pred[]{:T(512)S(6)} %compare.10), kind=kLoop, calls=%fused_computation.3.clone.1 | loop fusion | flops 1703936 | bytes 10223617 | tf_op jit(solution)/shard_map/while/body/eval_jaxpr/add | solution.py:105
  281.2 6.5 %subtract_convert_fusion = (bf16[256,3328]{1,0:T(8,128)(2,1)S(1)}, f32[256,3328]{1,0:T(8,128)}) fusion(f32[256,3328]{1,0:T(8,128)} %param.11, f32[]{:T(128)} %bitcast.15, f32[256,3328]{1,0:T(8,128)} %get-tuple-element.81, bf16[256,3328]{1,0:T(8,128)(2,1)} %param.13, f32[]{:T(128)} %bitcast.14, bf16[256,3328]{1,0:T(8,128)(2,1)} %param.12), kind=kLoop, calls=%fused_computation.15 | loop fusion | flops 15335424 | bytes 15335432 | tf_op jit(solution)/shard_map/convert_element_type | solution.py:116
  287.7 4.0 %collective-permute-start.7 = (bf16[256,256]{1,0:T(8,128)(2,1)S(1)}, bf16[256,256]{1,0:T(8,128)(2,1)S(1)}, u32[]{:S(2)}, u32[]{:S(2)}) collective-permute-start(bf16[256,256]{1,0:T(8,128)(2,1)S(1)} %get-tuple-element.120), channel_id=1, source_target_pairs={{0,1},{1,2},{2,3},{3,4},{4,5},{5,6},{6,7},{8,9},{9,10},{10,11},{11... | collective-permute-start | bytes 393224 | tf_op jit(solution)/shard_map/ppermute | solution.py:46
  291.8 1.9 collective-permute-start.8
  295.7 2.4 collective-permute-done.8
  298.0 3.1 %fusion.12 = bf16[256,3840]{1,0:T(8,128)(2,1)} fusion(s32[]{:T(128)S(6)} %select_n.47, bf16[256,256]{1,0:T(8,128)(2,1)S(1)} %collective-permute-done.7, bf16[256,3328]{1,0:T(8,128)(2,1)S(1)} %get-tuple-element.117, bf16[256,256]{1,0:T(8,128)(2,1)S(1)} %collective-permute-done.8, pred[3840]{0:T(1024)(128)(4,1)S(1)} %iota_compare_fusion, ...), kind=kLoop, calls=%fused_computation.23 | loop fusion | flops 8847360 | bytes 3943684 | tf_op jit(solution)/shard_map/jit(_where)/select_n | solution.py:79
  (22 shorter events, 3.4 us)
Async XLA Ops:
  7.2 203.0 %all-gather.2.cloned.1.call-start = ((), (), s32[]{:S(2)}) async-start(), calls=%async_computation.1 | async-start | bytes 28114944 | tf_op jit(solution)/shard_map/all_gather | solution.py:92
  31.9 7.0 %collective-permute-start = (bf16[512,256]{1,0:T(8,128)(2,1)S(1)}, bf16[512,256]{1,0:T(8,128)(2,1)S(1)}, u32[]{:S(2)}, u32[]{:S(2)}) collective-permute-start(bf16[512,256]{1,0:T(8,128)(2,1)S(1)} %bitcast.40), channel_id=1, source_target_pairs={{0,1},{1,2},{2,3},{3,4},{4,5},{5,6},{6,7},{7,0},{8,9},{9,10},{10,1... | collective-permute-start | bytes 786440 | tf_op jit(solution)/shard_map/ppermute | solution.py:29
  38.9 5.8 %collective-permute-start.1 = (bf16[512,256]{1,0:T(8,128)(2,1)S(1)}, bf16[512,256]{1,0:T(8,128)(2,1)S(1)}, u32[]{:S(2)}, u32[]{:S(2)}) collective-permute-start(bf16[512,256]{1,0:T(8,128)(2,1)S(1)} %collective-permute-done), channel_id=1, source_target_pairs={{0,1},{1,2},{2,3},{3,4},{4,5},{5,6},{6,7},{7,0},{8,9},{9,10},{10,1... | collective-permute-start | bytes 786440 | tf_op jit(solution)/shard_map/ppermute | solution.py:29
  41.3 6.2 %collective-permute-start.4 = (bf16[512,256]{1,0:T(8,128)(2,1)S(1)}, bf16[512,256]{1,0:T(8,128)(2,1)S(1)}, u32[]{:S(2)}, u32[]{:S(2)}) collective-permute-start(bf16[512,256]{1,0:T(8,128)(2,1)S(1)} %bitcast.41), channel_id=1, source_target_pairs={{1,0},{2,1},{3,2},{4,3},{5,4},{6,5},{7,6},{0,7},{9,8},{10,9},{11,1... | collective-permute-start | bytes 786440 | tf_op jit(solution)/shard_map/ppermute | solution.py:31
  44.7 5.8 %collective-permute-start.2 = (bf16[512,256]{1,0:T(8,128)(2,1)S(1)}, bf16[512,256]{1,0:T(8,128)(2,1)S(1)}, u32[]{:S(2)}, u32[]{:S(2)}) collective-permute-start(bf16[512,256]{1,0:T(8,128)(2,1)S(1)} %collective-permute-done.1), channel_id=1, source_target_pairs={{0,1},{1,2},{2,3},{3,4},{4,5},{5,6},{6,7},{7,0},{8,9},{9,10},{10,1... | collective-permute-start | bytes 786440 | tf_op jit(solution)/shard_map/ppermute | solution.py:29
  47.5 8.9 %collective-permute-start.5 = (bf16[512,256]{1,0:T(8,128)(2,1)S(1)}, bf16[512,256]{1,0:T(8,128)(2,1)}, u32[]{:S(2)}, u32[]{:S(2)}) collective-permute-start(bf16[512,256]{1,0:T(8,128)(2,1)S(1)} %collective-permute-done.4), channel_id=1, source_target_pairs={{1,0},{2,1},{3,2},{4,3},{5,4},{6,5},{7,6},{0,7},{9,8},{10,9},{11,1... | collective-permute-start | bytes 786440 | tf_op jit(solution)/shard_map/ppermute | solution.py:31
  50.5 8.5 %collective-permute-start.3 = (bf16[512,256]{1,0:T(8,128)(2,1)S(1)}, bf16[512,256]{1,0:T(8,128)(2,1)}, u32[]{:S(2)}, u32[]{:S(2)}) collective-permute-start(bf16[512,256]{1,0:T(8,128)(2,1)S(1)} %collective-permute-done.2), channel_id=1, source_target_pairs={{0,1},{1,2},{2,3},{3,4},{4,5},{5,6},{6,7},{7,0},{8,9},{9,10},{10,1... | collective-permute-start | bytes 786440 | tf_op jit(solution)/shard_map/ppermute | solution.py:29
  56.4 6.4 %collective-permute-start.6 = (bf16[512,256]{1,0:T(8,128)(2,1)}, bf16[512,256]{1,0:T(8,128)(2,1)S(1)}, u32[]{:S(2)}, u32[]{:S(2)}) collective-permute-start(bf16[512,256]{1,0:T(8,128)(2,1)} %collective-permute-done.5), channel_id=1, source_target_pairs={{1,0},{2,1},{3,2},{4,3},{5,4},{6,5},{7,6},{0,7},{9,8},{10,9},{11,1... | collective-permute-start | bytes 786440 | tf_op jit(solution)/shard_map/ppermute | solution.py:31
  287.7 8.0 %collective-permute-start.7 = (bf16[256,256]{1,0:T(8,128)(2,1)S(1)}, bf16[256,256]{1,0:T(8,128)(2,1)S(1)}, u32[]{:S(2)}, u32[]{:S(2)}) collective-permute-start(bf16[256,256]{1,0:T(8,128)(2,1)S(1)} %get-tuple-element.120), channel_id=1, source_target_pairs={{0,1},{1,2},{2,3},{3,4},{4,5},{5,6},{6,7},{8,9},{9,10},{10,11},{11... | collective-permute-start | bytes 393224 | tf_op jit(solution)/shard_map/ppermute | solution.py:46
  291.8 6.3 %collective-permute-start.8 = (bf16[256,256]{1,0:T(8,128)(2,1)S(1)}, bf16[256,256]{1,0:T(8,128)(2,1)S(1)}, u32[]{:S(2)}, u32[]{:S(2)}) collective-permute-start(bf16[256,256]{1,0:T(8,128)(2,1)S(1)} %get-tuple-element.119), channel_id=1, source_target_pairs={{1,0},{2,1},{3,2},{4,3},{5,4},{6,5},{7,6},{9,8},{10,9},{11,10},{12... | collective-permute-start | bytes 393224 | tf_op jit(solution)/shard_map/ppermute | solution.py:48
Sparse Core Ops, SparseCore 0:
  10.6 199.5 all-gather.1
